TPU v7x, 32 devices: a whole 2x2x4 slice. The times are simulated.
32 devices in a mesh: chan: 2 (over x), srow: 4 (over y, core), scol: 4 (over z).
Axes of the slice: x: 2, y: 2, z: 4, core: 2. Of those that a mesh axis runs over, the one named last changes fastest.
Arguments:
- vis: bfloat16 [2, 2, 512, 512], P('chan', None, 'srow', 'scol'), may hold values from -4 to 4
- model: bfloat16 [2, 64, 2, 512, 512], P('chan', None, None, 'srow', 'scol'), may hold values from -1 to 1, as said below
- flags: int32 [2, 32, 32], P('chan', 'srow', 'scol'), may hold values 0 or 1
- gains: float32 [2, 64, 2, 512], P('chan', None, None, ('srow', 'scol')), may hold values from -3 to 3
- consensus: float32 [64, 1, 2, 512], P(None, None, None, ('srow', 'scol')), may hold values from -3 to 3
- dual: float32 [2, 64, 2, 512], P('chan', None, None, ('srow', 'scol')), may hold values from -2 to 2
- rho: float32 [8], replicated, may hold values from 0.5 to 8
- cluster: int32 [64], replicated, may hold values from 0 to 7
Outputs:
- gains_out: float32 [2, 64, 2, 512], P('chan', None, None, ('srow', 'scol'))
- consensus_out: float32 [64, 1, 2, 512], P(None, None, None, ('srow', 'scol'))
- dual_out: float32 [2, 64, 2, 512], P('chan', None, None, ('srow', 'scol'))
Inputs may be any that keep to these rules, and one draw needn't show every extreme that they name: `model`: entries of about 1 / sqrt(512) in size.
All inputs are finite; a program needn't handle non-finite values. No bound on the sum of `flags` on one device may be relied on, other than what follows from the above.
Results may differ from a plain program's by a relative error of at most 0.0003.
Values sent between devices are 32-bit elements; how exact they have to be, the bound alone decides.
No kernel may reach another device: no remote copies, remote signals or barrier semaphores. Data moves between devices by JAX's collectives and lax.ppermute only.
A program may use at most 64 MiB of HBM per device.

v0:
```python
import math
import jax
import jax.numpy as jnp
from jax import lax
from jax.sharding import PartitionSpec as P

STATIONS = 512
TILE = 16
ITERS = 4
EPS = 1e-05
STEP = 0.5


def basis_table(groups, order):
    xval = (jnp.arange(groups, dtype=jnp.float32) + 0.5) / groups
    columns = [
        math.comb(order - 1, b) * xval**b * (1.0 - xval) ** (order - 1 - b) for b in range(order)
    ]
    return jnp.stack(columns, axis=1)


def local_terms(vis_block, model_block, weight, g_row, g_col):
    m_real = model_block[:, 0].astype(jnp.float32)
    m_imag = model_block[:, 1].astype(jnp.float32)
    c_real = g_col[:, 0][:, None, :]
    c_imag = g_col[:, 1][:, None, :]
    z_real = m_real * c_real + m_imag * c_imag
    z_imag = m_imag * c_real - m_real * c_imag
    r_real = g_row[:, 0][:, :, None]
    r_imag = g_row[:, 1][:, :, None]
    pred_real = jnp.sum(r_real * z_real - r_imag * z_imag, axis=0)
    pred_imag = jnp.sum(r_real * z_imag + r_imag * z_real, axis=0)
    res_real = vis_block[0].astype(jnp.float32) - pred_real
    res_imag = vis_block[1].astype(jnp.float32) - pred_imag
    w_real = weight * res_real
    w_imag = weight * res_imag
    power = jnp.sum(w_real * res_real + w_imag * res_imag)
    a_term = jnp.sum(weight[None] * (z_real * z_real + z_imag * z_imag), axis=-1)
    cross_real = jnp.sum(z_real * w_real[None] + z_imag * w_imag[None], axis=-1)
    cross_imag = jnp.sum(z_real * w_imag[None] - z_imag * w_real[None], axis=-1)
    return (power, a_term, jnp.stack([cross_real, cross_imag], axis=-2))


def solve(cross, a_term, g_now, target, rho_eff):
    denom = a_term + rho_eff[:, None]
    fresh = (cross + a_term[..., None, :] * g_now + rho_eff[:, None, None] * target) / denom[
        ..., None, :
    ]
    return g_now + STEP * (fresh - g_now)


def gram_solve(table, rhs):
    gram = jnp.dot(table.T, table, precision=lax.Precision.HIGHEST)
    factor = jnp.linalg.cholesky(gram)
    order = rhs.shape[1]
    flat = jnp.moveaxis(rhs, 1, 0).reshape(order, -1)
    sol = jax.scipy.linalg.cho_solve((factor, True), flat)
    return jnp.moveaxis(sol.reshape((order, rhs.shape[0]) + rhs.shape[2:]), 0, 1)


def sweep_terms(vis_block, model_block, weight, g_row, own_gains, rho_dir, groups):
    g_col = lax.all_gather(own_gains, "srow", axis=2, tiled=True)
    power, a_term, cross = local_terms(vis_block, model_block, weight, g_row, g_col)
    total = lax.psum(power, ("chan", "srow", "scol"))
    rho_eff = rho_dir * (total / (groups * STATIONS * STATIONS) + EPS)
    return (a_term, cross, rho_eff)


def shards(vis, model, flags, gains, consensus, dual, rho, cluster):
    groups = lax.axis_size("chan")
    order = consensus.shape[1]
    table = basis_table(groups, order)
    brow = lax.dynamic_index_in_dim(table, lax.axis_index("chan"), 0, keepdims=False)
    matches = cluster[:, None] == jnp.arange(rho.shape[0], dtype=jnp.int32)[None, :]
    rho_dir = jnp.sum(jnp.where(matches, rho[None, :], 0.0), axis=1)
    fl = flags[0].astype(jnp.float32)
    weight = jnp.repeat(jnp.repeat(fl, TILE, axis=0), TILE, axis=1)
    vis_block = vis[0]
    model_block = model[0]
    dual_own = dual[0]
    target = jnp.einsum("b,kbcp->kcp", brow, consensus, precision=lax.Precision.HIGHEST) - dual_own
    g = gains[0]
    for step in range(ITERS):
        g_row = lax.all_gather(g, "scol", axis=2, tiled=True)
        a_term, cross, rho_eff = sweep_terms(
            vis_block, model_block, weight, g_row, g, rho_dir, groups
        )
        a_own, cross_own = (
            lax.psum_scatter(a_term[:, None, :], "scol", scatter_dimension=2, tiled=True),
            lax.psum_scatter(cross, "scol", scatter_dimension=2, tiled=True),
        )
        g = solve(cross_own, a_own[:, 0, :], g, target, rho_eff)
    local = brow[None, :, None, None] * (g + dual_own)[:, None, :, :]
    sums = lax.psum(local, "chan")
    coeffs = gram_solve(table, sums)
    dual_new = (
        dual_own + g - jnp.einsum("b,kbcp->kcp", brow, coeffs, precision=lax.Precision.HIGHEST)
    )
    return (g[None], coeffs, dual_new[None])


def solution(mesh):
    placed = (
        P("chan", None, "srow", "scol"),
        P("chan", None, None, "srow", "scol"),
        P("chan", "srow", "scol"),
        P("chan", None, None, ("srow", "scol")),
        P(None, None, None, ("srow", "scol")),
        P("chan", None, None, ("srow", "scol")),
        P(),
        P(),
    )
    return jax.shard_map(
        shards,
        mesh=mesh,
        in_specs=placed,
        out_specs=(
            P("chan", None, None, ("srow", "scol")),
            P(None, None, None, ("srow", "scol")),
            P("chan", None, None, ("srow", "scol")),
        ),
        check_vma=False,
    )
```

profile of v0, /device:TPU:0, one launch (start us, length us, event | category | flops | bytes accessed | tf_op | source)
XLA Modules:
  0.0 436.5 jit_solution(12146551925661814514)
XLA Ops:
  7.2 15.3 %all-gather.1 = f32[1,64,2,128]{1,3,2,0:T(8,128)S(1)} all-gather(f32[1,64,2,32]{1,3,2,0:T(8,128)} %param.11), channel_id=3, replica_groups=mesh['chan'=2,'srow'=4,'scol'=4] {'scol'}, dimensions={3}, use_global_device_ids=true | all-gather | bytes 81920 | tf_op jit(solution)/shard_map/all_gather | solution.py:84
  22.5 5.6 %all-gather = f32[1,64,2,128]{1,3,2,0:T(8,128)S(1)} all-gather(f32[1,64,2,32]{1,3,2,0:T(8,128)} %param.11), channel_id=2, replica_groups=mesh['chan'=2,'srow'=4,'scol'=4] {'srow'}, dimensions={3}, use_global_device_ids=true | all-gather | bytes 81920 | tf_op jit(solution)/shard_map/all_gather | solution.py:62
  28.5 0.7 convert_bitcast_fusion
  29.6 6.2 %subtract_reduce_fusion.7 = (f32[128,128]{1,0:T(8,128)S(1)}, f32[128,128]{1,0:T(8,128)S(1)}) fusion(f32[64,128]{1,0:T(8,128)S(1)} %copy.125, f32[64,128]{1,0:T(8,128)S(1)} %copy.124, f32[64,128]{1,0:T(8,128)S(1)} %copy.122, f32[64,128]{1,0:T(8,128)S(1)} %copy.121, bf16[64,2,128,128]{3,2,1,0:T(8,128)(2,1)} %bitcast.195), kind=kLoop, calls=%fused_computation.43 | loop fusion | flops 16744448 | bytes 4456448 | tf_op jit(solution)/shard_map/reduce_sum | solution.py:31
  35.8 0.6 add_reduce_fusion.11
  36.4 4.1 add_reduce_fusion.6
  40.6 0.7 copy.130
  41.4 0.8 copy.128
  44.0 41.0 %psum.35 = f32[]{:T(128)} all-reduce(f32[]{:T(128)} %get-tuple-element.47), channel_id=1, replica_groups=mesh['chan'=2,'srow'=4,'scol'=4] {'chan','srow','scol'}, use_global_device_ids=true, to_apply=%region_9.10 | all-reduce | flops 1 | bytes 8 | tf_op jit(solution)/shard_map/psum | solution.py:64
  87.2 0.7 broadcast_add_fusion.3
  87.9 9.0 %all-reduce.9.cloned.1.call-done = f32[64,2,128]{0,1,2:T(2,128)} async-done(((f32[64,2,128]{0,1,2:T(2,128)}), f32[64,2,128]{0,1,2:T(2,128)}) %all-reduce.9.cloned.1.call-update) | async-done | bytes 65552
  96.9 0.9 bitcast_add_fusion.1
  97.8 13.5 %all_gather.27 = f32[64,2,128]{0,1,2:T(2,128)S(1)} all-gather(f32[64,2,32]{0,1,2:T(2,128)S(1)} %get-tuple-element.45), channel_id=1, replica_groups=mesh['chan'=2,'srow'=4,'scol'=4] {'scol'}, dimensions={2}, use_global_device_ids=true | all-gather | bytes 81920 | tf_op jit(solution)/shard_map/all_gather | solution.py:84
  111.3 5.4 %all_gather.26 = f32[64,2,128]{0,1,2:T(2,128)S(1)} all-gather(f32[64,2,32]{0,1,2:T(2,128)S(1)} %get-tuple-element.45), channel_id=1, replica_groups=mesh['chan'=2,'srow'=4,'scol'=4] {'srow'}, dimensions={2}, use_global_device_ids=true | all-gather | bytes 81920 | tf_op jit(solution)/shard_map/all_gather | solution.py:62
  117.3 6.2 %subtract_reduce_fusion.5 = (f32[128,128]{1,0:T(8,128)S(1)}, f32[128,128]{1,0:T(8,128)S(1)}) fusion(f32[64,128]{1,0:T(8,128)S(1)} %copy.136, f32[64,128]{1,0:T(8,128)S(1)} %copy.135, f32[64,128]{1,0:T(8,128)S(1)} %copy.134, f32[64,128]{1,0:T(8,128)S(1)} %copy.133, bf16[64,2,128,128]{3,2,1,0:T(8,128)(2,1)} %bitcast.196), kind=kLoop, calls=%fused_computation.38 | loop fusion | flops 16744448 | bytes 4456448 | tf_op jit(solution)/shard_map/reduce_sum | solution.py:31
  123.5 0.6 add_reduce_fusion.10
  124.1 4.1 add_reduce_fusion.4
  128.2 0.7 copy.140
  129.0 39.0 %psum.36 = f32[]{:T(128)} all-reduce(f32[]{:T(128)} %get-tuple-element.42), channel_id=1, replica_groups=mesh['chan'=2,'srow'=4,'scol'=4] {'chan','srow','scol'}, use_global_device_ids=true, to_apply=%region_18.19 | all-reduce | flops 1 | bytes 8 | tf_op jit(solution)/shard_map/psum | solution.py:64
  168.7 0.8 copy.139
  169.5 0.7 broadcast_add_fusion.2
  170.3 33.9 %all-reduce.11.cloned.1.call-done = f32[64,2,128]{0,1,2:T(2,128)} async-done(((f32[64,2,128]{0,1,2:T(2,128)}), f32[64,2,128]{0,1,2:T(2,128)}) %all-reduce.11.cloned.1.call-update) | async-done | bytes 65552
  204.2 0.8 multiply_add_fusion.2
  205.0 13.5 %all_gather.29 = f32[64,2,128]{0,1,2:T(2,128)S(1)} all-gather(f32[64,2,32]{0,1,2:T(2,128)S(1)} %multiply_add_fusion.2), channel_id=1, replica_groups=mesh['chan'=2,'srow'=4,'scol'=4] {'scol'}, dimensions={2}, use_global_device_ids=true | all-gather | bytes 81920 | tf_op jit(solution)/shard_map/all_gather | solution.py:84
  218.5 5.6 %all_gather.28 = f32[64,2,128]{0,1,2:T(2,128)S(1)} all-gather(f32[64,2,32]{0,1,2:T(2,128)S(1)} %multiply_add_fusion.2), channel_id=1, replica_groups=mesh['chan'=2,'srow'=4,'scol'=4] {'srow'}, dimensions={2}, use_global_device_ids=true | all-gather | bytes 81920 | tf_op jit(solution)/shard_map/all_gather | solution.py:62
  224.7 6.2 %subtract_reduce_fusion.3 = (f32[128,128]{1,0:T(8,128)S(1)}, f32[128,128]{1,0:T(8,128)S(1)}) fusion(f32[64,128]{1,0:T(8,128)S(1)} %copy.144, f32[64,128]{1,0:T(8,128)S(1)} %copy.143, f32[64,128]{1,0:T(8,128)S(1)} %copy.142, f32[64,128]{1,0:T(8,128)S(1)} %copy.141, bf16[64,2,128,128]{3,2,1,0:T(8,128)(2,1)} %bitcast.197), kind=kLoop, calls=%fused_computation.33 | loop fusion | flops 16744448 | bytes 4456448 | tf_op jit(solution)/shard_map/reduce_sum | solution.py:31
  230.9 0.6 add_reduce_fusion.9
  231.5 4.1 add_reduce_fusion.2
  235.6 0.7 copy.148
  236.4 38.9 %psum.37 = f32[]{:T(128)} all-reduce(f32[]{:T(128)} %get-tuple-element.39), channel_id=1, replica_groups=mesh['chan'=2,'srow'=4,'scol'=4] {'chan','srow','scol'}, use_global_device_ids=true, to_apply=%region_27.28 | all-reduce | flops 1 | bytes 8 | tf_op jit(solution)/shard_map/psum | solution.py:64
  276.0 0.8 copy.147
  276.9 0.7 broadcast_add_fusion.1
  277.6 33.9 %all-reduce.13.cloned.1.call-done = f32[64,2,128]{0,1,2:T(2,128)} async-done(((f32[64,2,128]{0,1,2:T(2,128)}), f32[64,2,128]{0,1,2:T(2,128)}) %all-reduce.13.cloned.1.call-update) | async-done | bytes 65552
  311.5 0.8 multiply_add_fusion.1
  312.3 13.6 %all_gather.31 = f32[64,2,128]{0,1,2:T(2,128)S(1)} all-gather(f32[64,2,32]{0,1,2:T(2,128)S(1)} %multiply_add_fusion.1), channel_id=1, replica_groups=mesh['chan'=2,'srow'=4,'scol'=4] {'scol'}, dimensions={2}, use_global_device_ids=true | all-gather | bytes 81920 | tf_op jit(solution)/shard_map/all_gather | solution.py:84
  325.9 5.4 %all_gather.30 = f32[64,2,128]{0,1,2:T(2,128)S(1)} all-gather(f32[64,2,32]{0,1,2:T(2,128)S(1)} %multiply_add_fusion.1), channel_id=1, replica_groups=mesh['chan'=2,'srow'=4,'scol'=4] {'srow'}, dimensions={2}, use_global_device_ids=true | all-gather | bytes 81920 | tf_op jit(solution)/shard_map/all_gather | solution.py:62
  331.8 6.2 %subtract_reduce_fusion.1 = (f32[128,128]{1,0:T(8,128)S(1)}, f32[128,128]{1,0:T(8,128)S(1)}) fusion(f32[64,128]{1,0:T(8,128)S(1)} %copy.152, f32[64,128]{1,0:T(8,128)S(1)} %copy.151, f32[64,128]{1,0:T(8,128)S(1)} %copy.150, f32[64,128]{1,0:T(8,128)S(1)} %copy.149, bf16[64,2,128,128]{3,2,1,0:T(8,128)(2,1)} %bitcast.198), kind=kLoop, calls=%fused_computation.28 | loop fusion | flops 16744448 | bytes 4456448 | tf_op jit(solution)/shard_map/reduce_sum | solution.py:31
  338.0 0.6 add_reduce_fusion.8
  338.6 4.1 add_reduce_fusion
  342.8 0.7 copy.156
  343.6 38.9 %psum.38 = f32[]{:T(128)} all-reduce(f32[]{:T(128)} %get-tuple-element.36), channel_id=1, replica_groups=mesh['chan'=2,'srow'=4,'scol'=4] {'chan','srow','scol'}, use_global_device_ids=true, to_apply=%region_36.37 | all-reduce | flops 1 | bytes 8 | tf_op jit(solution)/shard_map/psum | solution.py:64
  383.2 0.8 copy.155
  384.0 0.7 broadcast_add_fusion
  384.7 33.9 %all-reduce.15.cloned.1.call-done = f32[64,2,128]{0,1,2:T(2,128)} async-done(((f32[64,2,128]{0,1,2:T(2,128)}), f32[64,2,128]{0,1,2:T(2,128)}) %all-reduce.15.cloned.1.call-update) | async-done | bytes 65552
  418.6 0.8 fusion.21
  419.5 0.6 copy.157
  420.1 8.3 %psum.39 = f32[64,1,2,32]{0,2,3,1:T(2,128)S(1)} all-reduce(f32[64,1,2,32]{0,2,3,1:T(2,128)S(1)} %get-tuple-element.34), channel_id=1, replica_groups=mesh['chan'=2,'srow'=4,'scol'=4] {'chan'}, use_global_device_ids=true, to_apply=%region_37.38 | all-reduce | flops 4096 | bytes 32768 | tf_op jit(solution)/shard_map/psum | solution.py:94
  428.4 0.6 copy.158
  (84 shorter events, 4.8 us)
Async XLA Ops:
  7.2 28.6 %copy-start.4 = (bf16[1,2,128,128]{3,2,1,0:T(8,128)(2,1)S(1)}, bf16[1,2,128,128]{3,2,1,0:T(8,128)(2,1)}, u32[]{:S(2)}) copy-start(bf16[1,2,128,128]{3,2,1,0:T(8,128)(2,1)} %param.8) | copy-start | bytes 196612
  7.2 80.0 %reduce-scatter.5.cloned.1.call-start = ((), (), s32[]{:S(2)}) async-start(), calls=%async_computation.4 | async-start | bytes 81920 | tf_op jit(solution)/shard_map/reduce_scatter | solution.py:89
  29.5 6.9 %copy-start = (bf16[1,64,2,128,128]{4,3,2,1,0:T(8,128)(2,1)S(1)}, bf16[1,64,2,128,128]{4,3,2,1,0:T(8,128)(2,1)}, u32[]{:S(2)}) copy-start(bf16[1,64,2,128,128]{4,3,2,1,0:T(8,128)(2,1)} %param.9) | copy-start | bytes 12582916
  29.5 13.3 %copy-start.10 = (u32[32]{0:T(128)S(1)}, u32[32]{0:T(128)}, u32[]{:S(2)}) copy-start(u32[32]{0:T(128)} %constant.53) | copy-start | bytes 388
  29.5 56.8 %copy-start.8 = (f32[8]{0:T(128)S(1)}, f32[8]{0:T(128)}, u32[]{:S(2)}) copy-start(f32[8]{0:T(128)} %param.14) | copy-start | bytes 100
  29.5 56.8 %copy-start.9 = (s32[64]{0:T(128)S(1)}, s32[64]{0:T(128)}, u32[]{:S(2)}) copy-start(s32[64]{0:T(128)} %param.15) | copy-start | bytes 772
  29.6 67.4 %copy-start.5 = (f32[1,64,2,32]{1,3,2,0:T(8,128)S(1)}, f32[1,64,2,32]{1,3,2,0:T(8,128)}, u32[]{:S(2)}) copy-start(f32[1,64,2,32]{1,3,2,0:T(8,128)} %param.11) | copy-start | bytes 49156
  29.6 67.4 %copy-start.6 = (f32[1,64,2,32]{1,3,2,0:T(8,128)S(1)}, f32[1,64,2,32]{1,3,2,0:T(8,128)}, u32[]{:S(2)}) copy-start(f32[1,64,2,32]{1,3,2,0:T(8,128)} %param.13) | copy-start | bytes 49156
  29.6 67.3 %copy-start.7 = (f32[64,1,2,32]{0,3,2,1:T(8,128)S(1)}, f32[64,1,2,32]{0,3,2,1:T(8,128)}, u32[]{:S(2)}) copy-start(f32[64,1,2,32]{0,3,2,1:T(8,128)} %param.12) | copy-start | bytes 49156
  41.3 55.6 %all-reduce.9.cloned.1.call-start = ((), (), s32[]{:S(2)}) async-start(), calls=%async_computation.8 | async-start | bytes 262144
  42.1 127.4 %reduce-scatter.7.cloned.1.call-start = ((), (), s32[]{:S(2)}) async-start(), calls=%async_computation.5 | async-start | bytes 81920 | tf_op jit(solution)/shard_map/reduce_scatter | solution.py:89
  117.3 6.8 %copy-start.1 = (bf16[1,64,2,128,128]{4,3,2,1,0:T(8,128)(2,1)S(1)}, bf16[1,64,2,128,128]{4,3,2,1,0:T(8,128)(2,1)}, u32[]{:S(2)}) copy-start(bf16[1,64,2,128,128]{4,3,2,1,0:T(8,128)(2,1)} %param.9) | copy-start | bytes 12582916
  129.0 75.2 %all-reduce.11.cloned.1.call-start = ((), (), s32[]{:S(2)}) async-start(), calls=%async_computation.9 | async-start | bytes 262144
  169.5 107.4 %reduce-scatter.9.cloned.1.call-start = ((), (), s32[]{:S(2)}) async-start(), calls=%async_computation.6 | async-start | bytes 81920 | tf_op jit(solution)/shard_map/reduce_scatter | solution.py:89
  224.6 6.8 %copy-start.2 = (bf16[1,64,2,128,128]{4,3,2,1,0:T(8,128)(2,1)S(1)}, bf16[1,64,2,128,128]{4,3,2,1,0:T(8,128)(2,1)}, u32[]{:S(2)}) copy-start(bf16[1,64,2,128,128]{4,3,2,1,0:T(8,128)(2,1)} %param.9) | copy-start | bytes 12582916
  236.4 75.1 %all-reduce.13.cloned.1.call-start = ((), (), s32[]{:S(2)}) async-start(), calls=%async_computation.10 | async-start | bytes 262144
  276.8 107.2 %reduce-scatter.11.cloned.1.call-start = ((), (), s32[]{:S(2)}) async-start(), calls=%async_computation.7 | async-start | bytes 81920 | tf_op jit(solution)/shard_map/reduce_scatter | solution.py:89
  331.8 6.8 %copy-start.3 = (bf16[1,64,2,128,128]{4,3,2,1,0:T(8,128)(2,1)S(1)}, bf16[1,64,2,128,128]{4,3,2,1,0:T(8,128)(2,1)}, u32[]{:S(2)}) copy-start(bf16[1,64,2,128,128]{4,3,2,1,0:T(8,128)(2,1)} %param.9) | copy-start | bytes 12582916
  343.5 75.1 %all-reduce.15.cloned.1.call-start = ((), (), s32[]{:S(2)}) async-start(), calls=%async_computation.11 | async-start | bytes 262144
Sparse Core Ops, SparseCore 0:
  41.4 20.3 reduce-scatter.4
  64.2 32.6 all-reduce.8
  129.1 18.5 reduce-scatter.6
  169.6 34.5 all-reduce.10
  236.5 18.5 reduce-scatter.8
  276.9 34.5 all-reduce.12
  343.6 18.5 reduce-scatter.10
  384.1 34.5 all-reduce.14
where the time goes:
time: 438 us; the launch traced here: 437 us
  blocking collectives  244 us (56%)
  waiting for transfers between devices  111 us (25%)
  other arithmetic  51.5 us (12%)
  between operations  19.1 us (4%)
  local copies, waits for them, and re-layouts  10.6 us (2%)
    psum x4, blocking collectives, sweep_terms(): total = lax.psum(power, ('chan', 'srow', 'scol'))  158 us
    unnamed x12, waiting for transfers between devices  111 us
    all_gather x4, blocking collectives, shards(): g_row = lax.all_gather(g, 'scol', axis=2, tiled=True)  55.9 us
    reduce_sum x4, other arithmetic, local_terms(): pred_real = jnp.sum(r_real * z_real - r_imag * z_imag, axis=0)  24.7 us
    all_gather x4, blocking collectives, sweep_terms(): g_col = lax.all_gather(own_gains, 'srow', axis=2, tiled=True)  22 us
    reduce_sum x4, other arithmetic, local_terms(): cross_real = jnp.sum(z_real * w_real[None] + z_imag * w_imag[None], axis=-1)  16.5 us
  transfers between devices with their start and end apart: 8, of which 4 were waited for; matrix products, arithmetic and copies ran while one was open for 2% of the time, Pallas kernels for 0%

commit v1 on v0

--- a/solution.py
+++ b/solution.py
@@ -61,7 +61,7 @@
 def sweep_terms(vis_block, model_block, weight, g_row, own_gains, rho_dir, groups):
     g_col = lax.all_gather(own_gains, "srow", axis=2, tiled=True)
     power, a_term, cross = local_terms(vis_block, model_block, weight, g_row, g_col)
-    total = lax.psum(power, ("chan", "srow", "scol"))
+    total = jnp.sum(lax.all_gather(power, ("chan", "srow", "scol")), axis=0)
     rho_eff = rho_dir * (total / (groups * STATIONS * STATIONS) + EPS)
     return (a_term, cross, rho_eff)
 

time: 438 us -> 441 us (level)
    psum x4 -> x0, blocking collectives: 158 us -> none  [sweep_terms(): total = lax.psum(power, ('chan', 'srow', 'scol'))]
    unnamed x0 -> x4, blocking collectives: none -> 157 us
where the time goes in v1:
time: 441 us; the launch traced here: 439 us
  blocking collectives  243 us (55%)
  waiting for transfers between devices  110 us (25%)
  other arithmetic  53.9 us (12%)
  between operations  19.2 us (4%)
  local copies, waits for them, and re-layouts  13.6 us (3%)
    unnamed x4, blocking collectives  157 us
    unnamed x12, waiting for transfers between devices  109 us
    all_gather x4, blocking collectives, shards(): g_row = lax.all_gather(g, 'scol', axis=2, tiled=True)  55.9 us
    reduce_sum x4, other arithmetic, local_terms(): pred_real = jnp.sum(r_real * z_real - r_imag * z_imag, axis=0)  24.7 us
    all_gather x4, blocking collectives, sweep_terms(): g_col = lax.all_gather(own_gains, 'srow', axis=2, tiled=True)  22 us
    reduce_sum x4, other arithmetic, local_terms(): cross_real = jnp.sum(z_real * w_real[None] + z_imag * w_imag[None], axis=-1)  16.5 us
  transfers between devices with their start and end apart: 8, of which 4 were waited for; matrix products, arithmetic and copies ran while one was open for 2% of the time, Pallas kernels for 0%

profile of v1, /device:TPU:0, one launch (start us, length us, event | category | flops | bytes accessed | tf_op | source)
XLA Modules:
  0.0 439.4 jit_solution(3203869359259579303)
XLA Ops:
  7.2 15.3 %all-gather.1 = f32[1,64,2,128]{1,3,2,0:T(8,128)S(1)} all-gather(f32[1,64,2,32]{1,3,2,0:T(8,128)} %param.11), channel_id=3, replica_groups=mesh['chan'=2,'srow'=4,'scol'=4] {'scol'}, dimensions={3}, use_global_device_ids=true | all-gather | bytes 81920 | tf_op jit(solution)/shard_map/all_gather | solution.py:84
  22.5 5.6 %all-gather = f32[1,64,2,128]{1,3,2,0:T(8,128)S(1)} all-gather(f32[1,64,2,32]{1,3,2,0:T(8,128)} %param.11), channel_id=2, replica_groups=mesh['chan'=2,'srow'=4,'scol'=4] {'srow'}, dimensions={3}, use_global_device_ids=true | all-gather | bytes 81920 | tf_op jit(solution)/shard_map/all_gather | solution.py:62
  28.5 0.7 convert_bitcast_fusion
  29.6 6.2 %subtract_reduce_fusion.7 = (f32[128,128]{1,0:T(8,128)S(1)}, f32[128,128]{1,0:T(8,128)S(1)}) fusion(f32[64,128]{1,0:T(8,128)S(1)} %copy.125, f32[64,128]{1,0:T(8,128)S(1)} %copy.124, f32[64,128]{1,0:T(8,128)S(1)} %copy.122, f32[64,128]{1,0:T(8,128)S(1)} %copy.121, bf16[64,2,128,128]{3,2,1,0:T(8,128)(2,1)} %bitcast.199), kind=kLoop, calls=%fused_computation.43 | loop fusion | flops 16744448 | bytes 4456448 | tf_op jit(solution)/shard_map/reduce_sum | solution.py:31
  35.8 0.6 add_reduce_fusion.11
  36.4 4.1 add_reduce_fusion.6
  40.6 0.7 copy.130
  41.4 0.8 copy.128
  43.5 0.8 dynamic-update-slice.3
  44.8 40.5 %all-reduce = f32[32]{0:T(128)S(1)} all-reduce(f32[32]{0:T(128)S(1)} %dynamic-update-slice.3), channel_id=1, replica_groups=mesh['chan'=2,'srow'=4,'scol'=4] {'chan','srow','scol'}, use_global_device_ids=true, to_apply=%add | all-reduce | flops 32 | bytes 256
  88.1 0.7 broadcast_add_fusion.3
  88.8 8.1 %all-reduce.13.cloned.1.call-done = f32[64,2,128]{0,1,2:T(2,128)} async-done(((f32[64,2,128]{0,1,2:T(2,128)}), f32[64,2,128]{0,1,2:T(2,128)}) %all-reduce.13.cloned.1.call-update) | async-done | bytes 65552
  97.0 0.9 bitcast_add_fusion.1
  97.8 13.6 %all_gather.53 = f32[64,2,128]{0,1,2:T(2,128)S(1)} all-gather(f32[64,2,32]{0,1,2:T(2,128)S(1)} %get-tuple-element.45), channel_id=1, replica_groups=mesh['chan'=2,'srow'=4,'scol'=4] {'scol'}, dimensions={2}, use_global_device_ids=true | all-gather | bytes 81920 | tf_op jit(solution)/shard_map/all_gather | solution.py:84
  111.4 5.4 %all_gather.52 = f32[64,2,128]{0,1,2:T(2,128)S(1)} all-gather(f32[64,2,32]{0,1,2:T(2,128)S(1)} %get-tuple-element.45), channel_id=1, replica_groups=mesh['chan'=2,'srow'=4,'scol'=4] {'srow'}, dimensions={2}, use_global_device_ids=true | all-gather | bytes 81920 | tf_op jit(solution)/shard_map/all_gather | solution.py:62
  117.3 6.2 %subtract_reduce_fusion.5 = (f32[128,128]{1,0:T(8,128)S(1)}, f32[128,128]{1,0:T(8,128)S(1)}) fusion(f32[64,128]{1,0:T(8,128)S(1)} %copy.136, f32[64,128]{1,0:T(8,128)S(1)} %copy.135, f32[64,128]{1,0:T(8,128)S(1)} %copy.134, f32[64,128]{1,0:T(8,128)S(1)} %copy.133, bf16[64,2,128,128]{3,2,1,0:T(8,128)(2,1)} %bitcast.200), kind=kLoop, calls=%fused_computation.38 | loop fusion | flops 16744448 | bytes 4456448 | tf_op jit(solution)/shard_map/reduce_sum | solution.py:31
  123.5 0.6 add_reduce_fusion.10
  124.2 4.1 add_reduce_fusion.4
  128.3 0.7 copy.140
  129.0 0.8 dynamic-update-slice.4
  129.8 38.7 %all-reduce.1 = f32[32]{0:T(128)S(1)} all-reduce(f32[32]{0:T(128)S(1)} %dynamic-update-slice.4), channel_id=1, replica_groups=mesh['chan'=2,'srow'=4,'scol'=4] {'chan','srow','scol'}, use_global_device_ids=true, to_apply=%add.1 | all-reduce | flops 32 | bytes 256
  169.8 0.8 copy.139
  170.7 0.7 broadcast_add_fusion.2
  171.4 33.7 %all-reduce.15.cloned.1.call-done = f32[64,2,128]{0,1,2:T(2,128)} async-done(((f32[64,2,128]{0,1,2:T(2,128)}), f32[64,2,128]{0,1,2:T(2,128)}) %all-reduce.15.cloned.1.call-update) | async-done | bytes 65552
  205.1 0.8 multiply_add_fusion.2
  205.9 13.5 %all_gather.57 = f32[64,2,128]{0,1,2:T(2,128)S(1)} all-gather(f32[64,2,32]{0,1,2:T(2,128)S(1)} %multiply_add_fusion.2), channel_id=1, replica_groups=mesh['chan'=2,'srow'=4,'scol'=4] {'scol'}, dimensions={2}, use_global_device_ids=true | all-gather | bytes 81920 | tf_op jit(solution)/shard_map/all_gather | solution.py:84
  219.5 5.6 %all_gather.56 = f32[64,2,128]{0,1,2:T(2,128)S(1)} all-gather(f32[64,2,32]{0,1,2:T(2,128)S(1)} %multiply_add_fusion.2), channel_id=1, replica_groups=mesh['chan'=2,'srow'=4,'scol'=4] {'srow'}, dimensions={2}, use_global_device_ids=true | all-gather | bytes 81920 | tf_op jit(solution)/shard_map/all_gather | solution.py:62
  225.6 6.2 %subtract_reduce_fusion.3 = (f32[128,128]{1,0:T(8,128)S(1)}, f32[128,128]{1,0:T(8,128)S(1)}) fusion(f32[64,128]{1,0:T(8,128)S(1)} %copy.144, f32[64,128]{1,0:T(8,128)S(1)} %copy.143, f32[64,128]{1,0:T(8,128)S(1)} %copy.142, f32[64,128]{1,0:T(8,128)S(1)} %copy.141, bf16[64,2,128,128]{3,2,1,0:T(8,128)(2,1)} %bitcast.201), kind=kLoop, calls=%fused_computation.33 | loop fusion | flops 16744448 | bytes 4456448 | tf_op jit(solution)/shard_map/reduce_sum | solution.py:31
  232.5 4.1 add_reduce_fusion.2
  236.6 0.7 copy.148
  237.3 0.8 dynamic-update-slice.5
  238.1 38.7 %all-reduce.2 = f32[32]{0:T(128)S(1)} all-reduce(f32[32]{0:T(128)S(1)} %dynamic-update-slice.5), channel_id=1, replica_groups=mesh['chan'=2,'srow'=4,'scol'=4] {'chan','srow','scol'}, use_global_device_ids=true, to_apply=%add.2 | all-reduce | flops 32 | bytes 256
  278.1 0.8 copy.147
  279.0 0.7 broadcast_add_fusion.1
  279.7 33.7 %all-reduce.17.cloned.1.call-done = f32[64,2,128]{0,1,2:T(2,128)} async-done(((f32[64,2,128]{0,1,2:T(2,128)}), f32[64,2,128]{0,1,2:T(2,128)}) %all-reduce.17.cloned.1.call-update) | async-done | bytes 65552
  313.4 0.8 multiply_add_fusion.1
  314.2 13.5 %all_gather.61 = f32[64,2,128]{0,1,2:T(2,128)S(1)} all-gather(f32[64,2,32]{0,1,2:T(2,128)S(1)} %multiply_add_fusion.1), channel_id=1, replica_groups=mesh['chan'=2,'srow'=4,'scol'=4] {'scol'}, dimensions={2}, use_global_device_ids=true | all-gather | bytes 81920 | tf_op jit(solution)/shard_map/all_gather | solution.py:84
  327.8 5.4 %all_gather.60 = f32[64,2,128]{0,1,2:T(2,128)S(1)} all-gather(f32[64,2,32]{0,1,2:T(2,128)S(1)} %multiply_add_fusion.1), channel_id=1, replica_groups=mesh['chan'=2,'srow'=4,'scol'=4] {'srow'}, dimensions={2}, use_global_device_ids=true | all-gather | bytes 81920 | tf_op jit(solution)/shard_map/all_gather | solution.py:62
  333.7 6.2 %subtract_reduce_fusion.1 = (f32[128,128]{1,0:T(8,128)S(1)}, f32[128,128]{1,0:T(8,128)S(1)}) fusion(f32[64,128]{1,0:T(8,128)S(1)} %copy.152, f32[64,128]{1,0:T(8,128)S(1)} %copy.151, f32[64,128]{1,0:T(8,128)S(1)} %copy.150, f32[64,128]{1,0:T(8,128)S(1)} %copy.149, bf16[64,2,128,128]{3,2,1,0:T(8,128)(2,1)} %bitcast.202), kind=kLoop, calls=%fused_computation.28 | loop fusion | flops 16744448 | bytes 4456448 | tf_op jit(solution)/shard_map/reduce_sum | solution.py:31
  340.6 4.1 add_reduce_fusion
  344.7 0.7 copy.156
  345.4 0.8 dynamic-update-slice.6
  346.2 38.7 %all-reduce.3 = f32[32]{0:T(128)S(1)} all-reduce(f32[32]{0:T(128)S(1)} %dynamic-update-slice.6), channel_id=1, replica_groups=mesh['chan'=2,'srow'=4,'scol'=4] {'chan','srow','scol'}, use_global_device_ids=true, to_apply=%add.3 | all-reduce | flops 32 | bytes 256
  386.2 0.8 copy.155
  387.0 0.7 broadcast_add_fusion
  387.8 33.8 %all-reduce.19.cloned.1.call-done = f32[64,2,128]{0,1,2:T(2,128)} async-done(((f32[64,2,128]{0,1,2:T(2,128)}), f32[64,2,128]{0,1,2:T(2,128)}) %all-reduce.19.cloned.1.call-update) | async-done | bytes 65552
  421.5 0.8 fusion.21
  423.0 8.3 %psum.7 = f32[64,1,2,32]{0,2,3,1:T(2,128)S(1)} all-reduce(f32[64,1,2,32]{0,2,3,1:T(2,128)S(1)} %get-tuple-element.34), channel_id=1, replica_groups=mesh['chan'=2,'srow'=4,'scol'=4] {'chan'}, use_global_device_ids=true, to_apply=%region_37.38 | all-reduce | flops 4096 | bytes 32768 | tf_op jit(solution)/shard_map/psum | solution.py:94
  (96 shorter events, 9.7 us)
Async XLA Ops:
  7.2 28.6 %copy-start.4 = (bf16[1,2,128,128]{3,2,1,0:T(8,128)(2,1)S(1)}, bf16[1,2,128,128]{3,2,1,0:T(8,128)(2,1)}, u32[]{:S(2)}) copy-start(bf16[1,2,128,128]{3,2,1,0:T(8,128)(2,1)} %param.8) | copy-start | bytes 196612
  7.2 80.9 %reduce-scatter.5.cloned.1.call-start = ((), (), s32[]{:S(2)}) async-start(), calls=%async_computation.4 | async-start | bytes 81920 | tf_op jit(solution)/shard_map/reduce_scatter | solution.py:89
  29.5 6.9 %copy-start = (bf16[1,64,2,128,128]{4,3,2,1,0:T(8,128)(2,1)S(1)}, bf16[1,64,2,128,128]{4,3,2,1,0:T(8,128)(2,1)}, u32[]{:S(2)}) copy-start(bf16[1,64,2,128,128]{4,3,2,1,0:T(8,128)(2,1)} %param.9) | copy-start | bytes 12582916
  29.5 12.7 %copy-start.10 = (u32[32]{0:T(128)S(1)}, u32[32]{0:T(128)}, u32[]{:S(2)}) copy-start(u32[32]{0:T(128)} %constant.69) | copy-start | bytes 388
  29.5 57.2 %copy-start.8 = (f32[8]{0:T(128)S(1)}, f32[8]{0:T(128)}, u32[]{:S(2)}) copy-start(f32[8]{0:T(128)} %param.14) | copy-start | bytes 100
  29.5 57.2 %copy-start.9 = (s32[64]{0:T(128)S(1)}, s32[64]{0:T(128)}, u32[]{:S(2)}) copy-start(s32[64]{0:T(128)} %param.15) | copy-start | bytes 772
  29.6 67.4 %copy-start.5 = (f32[1,64,2,32]{1,3,2,0:T(8,128)S(1)}, f32[1,64,2,32]{1,3,2,0:T(8,128)}, u32[]{:S(2)}) copy-start(f32[1,64,2,32]{1,3,2,0:T(8,128)} %param.11) | copy-start | bytes 49156
  29.6 67.4 %copy-start.6 = (f32[1,64,2,32]{1,3,2,0:T(8,128)S(1)}, f32[1,64,2,32]{1,3,2,0:T(8,128)}, u32[]{:S(2)}) copy-start(f32[1,64,2,32]{1,3,2,0:T(8,128)} %param.13) | copy-start | bytes 49156
  29.6 67.4 %copy-start.7 = (f32[64,1,2,32]{0,3,2,1:T(8,128)S(1)}, f32[64,1,2,32]{0,3,2,1:T(8,128)}, u32[]{:S(2)}) copy-start(f32[64,1,2,32]{0,3,2,1:T(8,128)} %param.12) | copy-start | bytes 49156
  41.3 55.7 %all-reduce.13.cloned.1.call-start = ((), (), s32[]{:S(2)}) async-start(), calls=%async_computation.8 | async-start | bytes 262144
  42.1 128.5 %reduce-scatter.7.cloned.1.call-start = ((), (), s32[]{:S(2)}) async-start(), calls=%async_computation.5 | async-start | bytes 81920 | tf_op jit(solution)/shard_map/reduce_scatter | solution.py:89
  117.3 6.8 %copy-start.1 = (bf16[1,64,2,128,128]{4,3,2,1,0:T(8,128)(2,1)S(1)}, bf16[1,64,2,128,128]{4,3,2,1,0:T(8,128)(2,1)}, u32[]{:S(2)}) copy-start(bf16[1,64,2,128,128]{4,3,2,1,0:T(8,128)(2,1)} %param.9) | copy-start | bytes 12582916
  129.8 75.3 %all-reduce.15.cloned.1.call-start = ((), (), s32[]{:S(2)}) async-start(), calls=%async_computation.9 | async-start | bytes 262144
  170.6 108.4 %reduce-scatter.9.cloned.1.call-start = ((), (), s32[]{:S(2)}) async-start(), calls=%async_computation.6 | async-start | bytes 81920 | tf_op jit(solution)/shard_map/reduce_scatter | solution.py:89
  225.6 6.8 %copy-start.2 = (bf16[1,64,2,128,128]{4,3,2,1,0:T(8,128)(2,1)S(1)}, bf16[1,64,2,128,128]{4,3,2,1,0:T(8,128)(2,1)}, u32[]{:S(2)}) copy-start(bf16[1,64,2,128,128]{4,3,2,1,0:T(8,128)(2,1)} %param.9) | copy-start | bytes 12582916
  238.1 75.3 %all-reduce.17.cloned.1.call-start = ((), (), s32[]{:S(2)}) async-start(), calls=%async_computation.10 | async-start | bytes 262144
  278.9 108.1 %reduce-scatter.11.cloned.1.call-start = ((), (), s32[]{:S(2)}) async-start(), calls=%async_computation.7 | async-start | bytes 81920 | tf_op jit(solution)/shard_map/reduce_scatter | solution.py:89
  333.7 6.8 %copy-start.3 = (bf16[1,64,2,128,128]{4,3,2,1,0:T(8,128)(2,1)S(1)}, bf16[1,64,2,128,128]{4,3,2,1,0:T(8,128)(2,1)}, u32[]{:S(2)}) copy-start(bf16[1,64,2,128,128]{4,3,2,1,0:T(8,128)(2,1)} %param.9) | copy-start | bytes 12582916
  346.2 75.3 %all-reduce.19.cloned.1.call-start = ((), (), s32[]{:S(2)}) async-start(), calls=%async_computation.11 | async-start | bytes 262144
Sparse Core Ops, SparseCore 0:
  41.4 20.3 reduce-scatter.4
  64.2 32.6 all-reduce.12
  129.9 18.5 reduce-scatter.6
  170.7 34.3 all-reduce.14
  238.2 18.5 reduce-scatter.8
  279.0 34.3 all-reduce.16
  346.3 18.5 reduce-scatter.10
  387.1 34.3 all-reduce.18
